TPU v7x, 32 devices: a whole 2x2x4 slice. The times are simulated.
32 devices in a mesh: var: 4 (over x, core), space: 8 (over z, y).
Axes of the slice: x: 2, y: 2, z: 4, core: 2. Of those that a mesh axis runs over, the one named last changes fastest.
Arguments:
- fields: bfloat16 [8, 1024, 32768], P('var', None, 'space'), may hold values from -6 to 6
- eigenfunctions: bfloat16 [8, 64, 32768], P('var', None, 'space'), may hold values from -0.03125 to 0.03125
- start: float32 [512, 128], replicated, may hold values from -6 to 6
- grid_count: int32 [8], replicated, may hold values from 16384 to 32768
Outputs:
- loadings: bfloat16 [8, 128, 32768], P('var', None, 'space')
- component_scores: float32 [1024, 128], replicated
- explained: float32 [8, 1024], P('var')
Inputs may be any that keep to these rules, and one draw needn't show every extreme that they name: The grid of variable v is its points 0 to grid_count[v] - 1.
All inputs are finite; a program needn't handle non-finite values.
Results may differ from a plain program's by a relative error of at most 0.005.
Values sent between devices are 32-bit elements; how exact they have to be, the bound alone decides.
A program may use at most 64 MiB of HBM per device.

v0:
```python
import jax
import jax.numpy as jnp
from jax import lax
from jax.sharding import PartitionSpec as P

M = 64
SWEEPS = 2


def orthogonalize(image, gram):
    lower = jnp.linalg.cholesky(gram)
    return jax.scipy.linalg.solve_triangular(lower, image.T, lower=True).T


def product(left, right):
    return jnp.dot(left, right, precision=lax.Precision.HIGHEST, preferred_element_type=jnp.float32)


def shards(fields, eigenfunctions, start, grid_count):
    local_vars, samples, local_points = fields.shape
    first_var = lax.axis_index("var") * local_vars
    counts = lax.dynamic_slice_in_dim(grid_count, first_var, local_vars, 0)
    points = lax.axis_index("space") * local_points + jnp.arange(local_points, dtype=jnp.int32)
    valid = points[None, :] < counts[:, None]
    masked = jnp.where(valid[:, None, :], eigenfunctions, jnp.zeros((), eigenfunctions.dtype))
    part = jnp.einsum("vng,vmg->nvm", fields, masked, preferred_element_type=jnp.float32)
    summed = lax.psum(part.reshape(samples, local_vars * M), "space")
    joint = lax.all_gather(summed, "var", axis=1, tiled=True)
    centred = joint - jnp.mean(joint, axis=0, keepdims=True)
    basis = start
    cov = product(centred.T, centred) / (samples - 1)
    for sweep in range(SWEEPS):
        image = product(cov, basis)
        basis = orthogonalize(image, product(image.T, image))
    component_scores = product(centred, basis)
    scores_low = component_scores.astype(jnp.bfloat16)
    own_basis = lax.dynamic_slice_in_dim(basis, first_var * M, local_vars * M, 0)
    basis_low = own_basis.astype(jnp.bfloat16).reshape(local_vars, M, basis.shape[1])
    loadings = jnp.einsum(
        "vmk,vmg->vkg", basis_low, masked, preferred_element_type=jnp.float32
    ).astype(jnp.bfloat16)
    partial_gain = []
    for local in range(local_vars):
        rebuilt = jnp.dot(scores_low, loadings[local], preferred_element_type=jnp.float32)
        wide = fields[local].astype(jnp.float32)
        deviation = wide - jnp.mean(wide, axis=0, keepdims=True)
        partial_gain.append(jnp.sum(2.0 * deviation * rebuilt - rebuilt * rebuilt, axis=1) / M)
    explained = lax.psum(jnp.stack(partial_gain, axis=0), "space")
    return (loadings, component_scores, explained)


def solution(mesh):
    return jax.shard_map(
        shards,
        mesh=mesh,
        in_specs=(P("var", None, "space"), P("var", None, "space"), P(), P()),
        out_specs=(P("var", None, "space"), P(), P("var", None)),
        check_vma=False,
    )
```

profile of v0, /device:TPU:0, one launch (start us, length us, event | category | flops | bytes accessed | tf_op | source)
XLA Modules:
  0.0 234.2 jit_solution(11181255422536817181)
XLA Ops:
  7.2 0.7 dynamic_slice.6
  8.1 12.1 %fusion.19 = f32[2,64,1024]{2,1,0:T(8,128)} fusion(bf16[2,1024,4096]{2,1,0:T(8,128)(2,1)} %param.7, bf16[2,64,4096]{2,1,0:T(8,128)(2,1)} %param.8, pred[2,4096]{1,0:T(4,128)(4,1)S(1)} %broadcast_compare_fusion), kind=kOutput, calls=%fused_computation.25 | convolution fusion | flops 1074266112 | bytes 18358272 | tf_op jit(solution)/shard_map/vng,vmg->nvm/dot_general | solution.py:26
  20.2 75.6 %all-reduce.2.cloned.1.call-done = f32[1024,128]{0,1:T(8,128)} async-done(((f32[1024,128]{0,1:T(8,128)}), f32[1024,128]{0,1:T(8,128)}) %all-reduce.2.cloned.1.call-update) | async-done | bytes 524304 | tf_op jit(solution)/shard_map/psum | solution.py:27
  95.9 7.8 %convert_reduce_fusion.1 = (f32[4096]{0:T(1024)S(1)}, f32[4096]{0:T(1024)S(1)}) fusion(bf16[2,1024,4096]{2,1,0:T(8,128)(2,1)} %param.7), kind=kLoop, calls=%fused_computation.2 | loop fusion | flops 16769024 | bytes 16809984 | tf_op jit(solution)/shard_map/reduce_sum | solution.py:46
  104.2 14.9 %all-gather.2.cloned.1.call-done = f32[1024,512]{0,1:T(8,128)} async-done(((f32[1024,128]{0,1:T(8,128)}), f32[1024,512]{0,1:T(8,128)}) %all-gather.2.cloned.1.call-update) | async-done | bytes 2097168 | tf_op jit(solution)/shard_map/all_gather | solution.py:28
  119.2 1.9 reduce_sum.45
  121.1 5.9 %fusion.14 = f32[512,512]{1,0:T(8,128)S(1)} fusion(f32[1024,512]{0,1:T(8,128)} %all-gather.2.cloned.1.call-done, f32[512]{0:T(512)S(1)} %broadcast_multiply_fusion.4), kind=kOutput, calls=%fused_computation.19 | convolution fusion | flops 3222011904 | bytes 3147776 | tf_op jit(solution)/shard_map/dot_general | solution.py:16
  127.0 1.0 copy-done.3
  128.0 1.0 fusion.39
  129.0 0.7 copy-done.5
  131.0 12.5 %cholesky.44 = f32[128,128]{1,0:T(8,128)S(1)} custom-call(f32[128,128]{1,0:T(8,128)} %fusion.33), custom_call_target="Cholesky" | custom-call | tf_op jit(solution)/shard_map/jit(cholesky)/cholesky | solution.py:11
  144.9 9.8 %custom-call.6 = f32[1,128,128]{1,2,0:T(8,128)S(1)} custom-call(f32[1,128,128]{2,1,0:T(8,128)S(1)} %fusion.28), custom_call_target="InvertDiagBlocksLowerTriangular" | custom-call | tf_op jit(solution)/shard_map/jit(_solve_triangular)/triangular_solve | solution.py:12
  154.7 1.4 fusion.24
  156.1 2.5 %fusion.41 = f32[512,128]{1,0:T(8,128)S(1)} fusion(f32[512,512]{1,0:T(8,128)} %copy-done.3, f32[128,512]{1,0:T(8,128)S(1)} %fusion.24), kind=kOutput, calls=%fused_computation.65 | convolution fusion | flops 402653184 | bytes 1572864 | tf_op jit(solution)/shard_map/dot_general | solution.py:16
  158.6 0.7 copy-done.4
  160.6 12.5 %cholesky.55 = f32[128,128]{1,0:T(8,128)S(1)} custom-call(f32[128,128]{1,0:T(8,128)} %fusion.31), custom_call_target="Cholesky" | custom-call | tf_op jit(solution)/shard_map/jit(cholesky)/cholesky | solution.py:11
  174.5 9.8 %custom-call.7 = f32[1,128,128]{1,2,0:T(8,128)S(1)} custom-call(f32[1,128,128]{2,1,0:T(8,128)S(1)} %fusion.29), custom_call_target="InvertDiagBlocksLowerTriangular" | custom-call | tf_op jit(solution)/shard_map/jit(_solve_triangular)/triangular_solve | solution.py:12
  184.3 1.4 fusion.22
  186.5 0.8 convolution_convert_fusion
  187.3 4.7 %fusion.10 = f32[1024,128]{1,0:T(8,128)S(1)} fusion(f32[128,512]{1,0:T(8,128)} %copy-done.7, f32[1024,512]{0,1:T(8,128)S(1)} %copy-done.2, f32[512]{0:T(512)} %copy-done.10), kind=kOutput, calls=%fused_computation.15 | convolution fusion | flops 805830656 | bytes 2885632 | tf_op jit(solution)/shard_map/dot_general | solution.py:16
  192.1 7.2 %fusion.9 = f32[1024]{0:T(1024)S(1)} fusion(f32[4096]{0:T(1024)} %get-tuple-element.7, bf16[2,1024,4096]{2,1,0:T(8,128)(2,1)} %param.7, bf16[2,128,4096]{2,1,0:T(8,128)(2,1)S(1)} %convolution_convert_fusion, f32[1024,128]{1,0:T(8,128)S(1)} %fusion.10), kind=kOutput, calls=%fused_computation.13 | convolution fusion | flops 1103232000 | bytes 9981952 | tf_op jit(solution)/shard_map/dot_general | solution.py:44
  199.4 1.2 slice-done.3
  200.5 4.5 %fusion.4 = f32[1024]{0:T(1024)S(1)} fusion(f32[4096]{0:T(1024)S(1)} %copy-done.9, bf16[2,1024,4096]{2,1,0:T(8,128)(2,1)S(1)} %bitcast.74, bf16[2,128,4096]{2,1,0:T(8,128)(2,1)S(1)} %convolution_convert_fusion, f32[1024,128]{1,0:T(8,128)S(1)} %fusion.10), kind=kOutput, calls=%fused_computation.8 | convolution fusion | flops 1103232000 | bytes 9981952 | tf_op jit(solution)/shard_map/dot_general | solution.py:44
  205.2 22.2 %psum.15 = f32[2,1024]{1,0:T(2,128)} all-reduce(f32[2,1024]{1,0:T(2,128)S(1)} %pad_maximum_fusion), channel_id=1, replica_groups=mesh['var'=4,'space'=8] {'space'}, use_global_device_ids=true, to_apply=%region_8.11 | all-reduce | flops 2048 | bytes 16384 | tf_op jit(solution)/shard_map/psum | solution.py:48
  (52 shorter events, 7.0 us)
Async XLA Ops:
  7.2 120.8 %copy-start = (f32[512,128]{1,0:T(8,128)S(1)}, f32[512,128]{1,0:T(8,128)}, u32[]{:S(2)}) copy-start(f32[512,128]{1,0:T(8,128)} %param.9) | copy-start | bytes 786436
  7.2 88.6 %all-reduce.2.cloned.1.call-start = ((), (), s32[]{:S(2)}) async-start(), calls=%async_computation | async-start | bytes 1048576 | tf_op jit(solution)/shard_map/psum | solution.py:27
  20.2 166.4 %copy-start.1 = (bf16[2,64,4096]{2,1,0:T(8,128)(2,1)S(1)}, bf16[2,64,4096]{2,1,0:T(8,128)(2,1)}, u32[]{:S(2)}) copy-start(bf16[2,64,4096]{2,1,0:T(8,128)(2,1)} %param.8) | copy-start | bytes 3145732
  20.2 99.0 %all-gather.2.cloned.1.call-start = ((), (), s32[]{:S(2)}) async-start(), calls=%async_computation.1 | async-start | bytes 2621440 | tf_op jit(solution)/shard_map/all_gather | solution.py:28
  119.2 68.1 %copy-start.2 = (f32[1024,512]{0,1:T(8,128)S(1)}, f32[1024,512]{0,1:T(8,128)}, u32[]{:S(2)}) copy-start(f32[1024,512]{0,1:T(8,128)} %all-gather.2.cloned.1.call-done) | copy-start | bytes 6291460
  121.1 5.9 %copy-start.10 = (f32[512]{0:T(512)}, f32[512]{0:T(512)S(1)}, u32[]{:S(2)}) copy-start(f32[512]{0:T(512)S(1)} %broadcast_multiply_fusion.4) | copy-start | bytes 6148
  127.0 1.0 copy-start.3
  129.0 0.7 copy-start.5
  158.6 0.7 copy-start.4
  185.7 0.7 copy-start.7
  187.3 12.0 %copy-start.6 = (bf16[2,128,4096]{2,1,0:T(8,128)(2,1)}, bf16[2,128,4096]{2,1,0:T(8,128)(2,1)S(1)}, u32[]{:S(2)}) copy-start(bf16[2,128,4096]{2,1,0:T(8,128)(2,1)S(1)} %convolution_convert_fusion) | copy-start | bytes 6291460
  192.0 13.1 %copy-start.8 = (f32[1024,128]{1,0:T(8,128)}, f32[1024,128]{1,0:T(8,128)S(1)}, u32[]{:S(2)}) copy-start(f32[1024,128]{1,0:T(8,128)S(1)} %fusion.10) | copy-start | bytes 1572868
  192.0 7.3 %slice-start = ((s8[16777216]{0:T(1024)(128)(4,1)}), s8[4194304]{0:T(1024)(128)(4,1)S(1)}, s32[]{:S(2)}) async-start(s8[16777216]{0:T(1024)(128)(4,1)} %bitcast.73), calls=%async_computation.2 | async-start | bytes 8388608
  192.0 7.3 %copy-start.9 = (f32[4096]{0:T(1024)S(1)}, f32[4096]{0:T(1024)}, u32[]{:S(2)}) copy-start(f32[4096]{0:T(1024)} %get-tuple-element.8) | copy-start | bytes 49156
  192.0 7.3 %slice-start.1 = ((s8[16777216]{0:T(1024)(128)(4,1)}), s8[4194304]{0:T(1024)(128)(4,1)S(1)}, s32[]{:S(2)}) async-start(s8[16777216]{0:T(1024)(128)(4,1)} %bitcast.73), calls=%async_computation.3 | async-start | bytes 8388608
  192.1 7.3 %slice-start.2 = ((s8[16777216]{0:T(1024)(128)(4,1)}), s8[4194304]{0:T(1024)(128)(4,1)S(1)}, s32[]{:S(2)}) async-start(s8[16777216]{0:T(1024)(128)(4,1)} %bitcast.73), calls=%async_computation.4 | async-start | bytes 8388608
  192.1 8.5 %slice-start.3 = ((s8[16777216]{0:T(1024)(128)(4,1)}), s8[4194304]{0:T(1024)(128)(4,1)S(1)}, s32[]{:S(2)}) async-start(s8[16777216]{0:T(1024)(128)(4,1)} %bitcast.73), calls=%async_computation.5 | async-start | bytes 8388608
Sparse Core Ops, SparseCore 0:
  20.3 75.4 all-reduce.1
  97.4 21.7 all-gather.1
where the time goes:
time: 235 us; the launch traced here: 234 us
  waiting for transfers between devices  90.5 us (39%)
  other arithmetic  59 us (25%)
  matrix products  42.6 us (18%)
  blocking collectives  22.2 us (9%)
  between operations  14.4 us (6%)
  local copies, waits for them, and re-layouts  5.37 us (2%)
    psum x1, waiting for transfers between devices, shards(): summed = lax.psum(part.reshape(samples, local_vars * M), 'space')  75.6 us
    another operation x6, other arithmetic, orthogonalize(): lower = jnp.linalg.cholesky(gram)  26.4 us
    psum x1, blocking collectives, shards(): explained = lax.psum(jnp.stack(partial_gain, axis=0), 'space')  22.2 us
    another operation x4, other arithmetic, orthogonalize(): return jax.scipy.linalg.solve_triangular(lower, image.T, lower=True).T  20.9 us
    dot_general x6, matrix products, product(): jnp.dot(left, right, precision=lax.Precision.HIGHEST, preferred_element_t...  15.2 us
    all_gather x1, waiting for transfers between devices, shards(): joint = lax.all_gather(summed, 'var', axis=1, tiled=True)  14.9 us
    dot_general x1, matrix products, shards(): jnp.einsum('vng,vmg->nvm', fields, masked, preferred_element_type=jnp.flo...  12.1 us
    dot_general x2, matrix products, shards(): jnp.dot(scores_low, loadings[local], preferred_element_type=jnp.float32)  11.8 us
  transfers between devices with their start and end apart: 2, of which 2 were waited for; matrix products, arithmetic and copies ran while one was open for 4% of the time, Pallas kernels for 0%

commit v1 on v0

v1 whole, which is shorter than its diff:
```python
import functools

import jax
import jax.numpy as jnp
from jax import lax
from jax.experimental import pallas as pl
from jax.experimental.pallas import tpu as pltpu
from jax.sharding import PartitionSpec as P

M = 64
SWEEPS = 2
MESH = pl.DeviceIdType.MESH
F32 = jnp.float32
BF16 = jnp.bfloat16
HIGHEST = lax.Precision.HIGHEST


def dot(left, right, dims, precision=None):
    return lax.dot_general(left, right, (dims, ((), ())), precision=precision, preferred_element_type=F32)


NN = ((1,), (0,))
NT = ((1,), (1,))
TN = ((0,), (0,))


def split(x):
    high = x.astype(BF16)
    return high, (x - high.astype(F32)).astype(BF16)


def dot3(left, right, dims):
    (lh, ll), (rh, rl) = left, right
    return dot(lh, rh, dims) + (dot(lh, rl, dims) + dot(ll, rh, dims))


def remote(src, dst, send, recv, target):
    return pltpu.make_async_remote_copy(
        src_ref=src, dst_ref=dst, send_sem=send, recv_sem=recv, device_id=target, device_id_type=MESH
    )


def gather_kernel(
    n, nv, fields, masked, centred_ref, gram_ref,
    fbuf, part, rbuf, red, gpart, grbuf, gred, gfull, jbuf,
    fsem, asend, arecv, gsend, grecv, bsend, brecv, csend, crecv, dsend, drecv, hsend, hrecv,
):
    var, me = lax.axis_index("var"), lax.axis_index("space")
    local_vars, samples, _ = fields.shape
    rows = samples // n
    width = local_vars * M
    own_columns = pl.ds(pl.multiple_of(var * width, width), width)
    partner = var + 1 - 2 * (var % 2)
    half = rows // 2

    def at(i):
        return lax.rem(me + 1 + i, n)

    def fetch(i):
        block = pl.ds(pl.multiple_of(at(i) * rows, rows), rows)
        slot = lax.rem(i, 3)
        return pltpu.make_async_copy(fields.at[:, block, :], fbuf.at[slot], fsem.at[slot])

    fetch(0).start()
    fetch(1).start()

    barrier = pltpu.get_barrier_semaphore()
    for d in range(1, n):
        pl.semaphore_signal(barrier, inc=1, device_id=(var, lax.rem(me + d, n)), device_id_type=MESH)
    for d in range(1, nv):
        pl.semaphore_signal(barrier, inc=1, device_id=(lax.rem(var + d, nv), me), device_id_type=MESH)

    gram = jnp.concatenate([dot(masked[v], masked[v], NT) for v in range(local_vars)], axis=1)
    grows = M // n
    gpart[...] = jnp.zeros_like(gpart)
    for s in range(n):
        gpart[s, 0:grows, :] = gram[s * grows:(s + 1) * grows, :]

    pl.semaphore_wait(barrier, n - 1 + nv - 1)

    def send_part(i):
        return remote(part.at[i], rbuf.at[i], asend.at[i], arecv.at[i], (var, at(i)))

    def send_gram(i):
        return remote(gpart.at[at(i)], grbuf.at[i], gsend.at[i], grecv.at[i], (var, at(i)))

    def step(i, carry):
        slot = lax.rem(i, 3)

        @pl.when(i + 2 < n)
        def _():
            fetch(i + 2).start()

        @pl.when(i > 0)
        def _():
            send_part(i - 1).start()
            send_gram(i - 1).start()

        fetch(i).wait()
        part[i] = jnp.concatenate(
            [dot(fbuf[slot, v], masked[v], NT) for v in range(local_vars)], axis=1
        )
        return carry

    lax.fori_loop(0, n, step, 0)

    def wait_part(i, carry):
        send_part(i).wait()
        send_gram(i).wait()
        return carry

    lax.fori_loop(0, n - 1, wait_part, 0)

    total = part[n - 1]
    gtotal = gpart[me]
    for i in range(n - 1):
        total = total + rbuf[i]
        gtotal = gtotal + grbuf[i]
    red[...] = total
    gred[...] = gtotal
    own_rows = pl.ds(pl.multiple_of(me * rows, rows), rows)
    jbuf[own_rows, own_columns] = total
    gfull[me] = gtotal

    def send_columns(d):
        return remote(
            red, jbuf.at[own_rows, own_columns], bsend.at[d - 1], brecv.at[d - 1], (lax.rem(var + d, nv), me)
        )

    def send_gfull(d):
        return remote(gred, gfull.at[me], hsend.at[d - 1], hrecv.at[d - 1], (var, lax.rem(me + d, n)))

    for d in range(1, nv):
        send_columns(d).start()
    for d in range(1, nv):
        send_columns(d).wait()

    def half_block(s):
        return jbuf.at[pl.ds(pl.multiple_of(s * rows + lax.rem(var, 2) * half, half), half), :]

    def send_rows(d):
        return remote(half_block(me), half_block(me), csend.at[d - 1], crecv.at[d - 1], (var, lax.rem(me + d, n)))

    def pass_on(d):
        source = lax.rem(me - d + n, n)
        return remote(half_block(source), half_block(source), dsend.at[d - 1], drecv.at[d - 1], (partner, me))

    for d in range(1, n):
        send_rows(d).start()
    for d in range(1, n):
        send_gfull(d).start()
    for d in range(1, n):
        send_rows(d).wait_recv()
        pass_on(d).start()
    for d in range(1, n):
        send_gfull(d).wait()
        send_rows(d).wait_send()
    for d in range(1, n):
        pass_on(d).wait()

    mean = jnp.sum(jbuf[...], axis=0, keepdims=True) / samples
    centred_ref[...] = jbuf[...] - mean
    for s in range(n):
        gram_ref[s * grows:(s + 1) * grows, :] = gfull[s, 0:grows, :]


def gather_scores(n, nv, fields, masked):
    local_vars, samples, points = fields.shape
    rows = samples // n
    width = local_vars * M
    dma = pltpu.SemaphoreType.DMA
    return pl.pallas_call(
        functools.partial(gather_kernel, n, nv),
        out_shape=(
            jax.ShapeDtypeStruct((samples, nv * width), F32),
            jax.ShapeDtypeStruct((M, width), F32),
        ),
        in_specs=[pl.BlockSpec(memory_space=pl.ANY), pl.BlockSpec(memory_space=pltpu.VMEM)],
        out_specs=(pl.BlockSpec(memory_space=pltpu.VMEM), pl.BlockSpec(memory_space=pltpu.VMEM)),
        scratch_shapes=[
            pltpu.VMEM((3, local_vars, rows, points), BF16),
            pltpu.VMEM((n, rows, width), F32),
            pltpu.VMEM((n - 1, rows, width), F32),
            pltpu.VMEM((rows, width), F32),
            pltpu.VMEM((n, 8, width), F32),
            pltpu.VMEM((n - 1, 8, width), F32),
            pltpu.VMEM((8, width), F32),
            pltpu.VMEM((n, 8, width), F32),
            pltpu.VMEM((samples, nv * width), F32),
            dma((3,)),
            dma((n - 1,)), dma((n - 1,)),
            dma((n - 1,)), dma((n - 1,)),
            dma((nv - 1,)), dma((nv - 1,)),
            dma((n - 1,)), dma((n - 1,)),
            dma((n - 1,)), dma((n - 1,)),
            dma((n - 1,)), dma((n - 1,)),
        ],
        compiler_params=pltpu.CompilerParams(
            collective_id=0, has_side_effects=True, vmem_limit_bytes=48 * 1024 * 1024
        ),
        name="gather_scores",
    )(fields, masked)


def inverse_factor(gram):
    size = gram.shape[0]
    tiles = size // 8
    rows = [gram[8 * i:8 * i + 8, :] for i in range(tiles)]
    lane = lax.broadcasted_iota(jnp.int32, (1, size), 1)
    lane8 = lax.broadcasted_iota(jnp.int32, (8, size), 1)
    sublane = lax.broadcasted_iota(jnp.int32, (8, size), 0)
    done = []
    for k in range(size):
        tile, at = k // 8, k % 8
        columns = {i: jnp.broadcast_to(rows[i][:, k:k + 1], (8, size)) for i in range(tile, tiles)}
        pivot = columns[tile][at:at + 1, :]
        row = jnp.where(lane == k, 1.0, rows[tile][at:at + 1, :])
        done.append(jnp.where(lane <= k, row, 0.0) * lax.rsqrt(pivot))
        scaled = jnp.broadcast_to(row * (1.0 / pivot), (8, size))
        for i in range(tile, tiles):
            new = jnp.where(lane8 == k, 0.0, rows[i]) - columns[i] * scaled
            rows[i] = jnp.where(sublane > at, new, rows[i]) if i == tile else new
    return done


def basis_kernel(
    centred_ref, gram_ref, start_ref, masked_ref, loadings_ref, scores_ref, explained_ref,
    high_ref, low_ref, cov_high, cov_low, basis_ref, inverse_ref,
):
    var = lax.axis_index("var")
    samples = centred_ref.shape[0]
    local_vars = masked_ref.shape[0]
    width = local_vars * M
    high, low = split(centred_ref[...])
    high_ref[...] = high
    low_ref[...] = low
    cov = dot3((high, low), (high, low), TN) / (samples - 1)
    cov_high[...], cov_low[...] = split(cov)
    basis_ref[...] = start_ref[...]

    def sweep(_, carry):
        image = dot3((cov_high[...], cov_low[...]), split(basis_ref[...]), NN)
        gram = dot(image, image, TN, HIGHEST)
        for k, row in enumerate(inverse_factor(gram)):
            inverse_ref[k:k + 1, :] = row
        basis_ref[...] = dot(image, inverse_ref[...], NT, HIGHEST)
        return carry

    lax.fori_loop(0, SWEEPS, sweep, 0)

    scores = dot3((high_ref[...], low_ref[...]), split(basis_ref[...]), NN)
    scores_ref[...] = scores
    scores_low = scores.astype(BF16)
    own = pl.ds(pl.multiple_of(var * width, width), width)
    basis_low = basis_ref[own, :].astype(BF16)
    own_high, own_low = high_ref[:, own], low_ref[:, own]
    ones = jnp.ones((8, basis_low.shape[1]), F32)
    scores_wide = scores_low.astype(F32)
    for v in range(local_vars):
        mine = basis_low[v * M:(v + 1) * M, :]
        loadings_ref[v] = dot(mine, masked_ref[v], TN).astype(BF16)
        left, right = own_high[:, v * M:(v + 1) * M], own_low[:, v * M:(v + 1) * M]
        cross = dot(left, mine, NN) + dot(right, mine, NN)
        wide = mine.astype(F32)
        inner = dot(gram_ref[:, v * M:(v + 1) * M], wide, NN, HIGHEST)
        square = split(dot(wide, inner, TN, HIGHEST))
        quad = dot(scores_low, square[0], NN) + dot(scores_low, square[1], NN)
        gain = scores_wide * (2.0 * cross - quad)
        summed = dot(ones, gain, NT, HIGHEST) / M
        explained_ref[v:v + 1, :] = summed[0:1, :]


def finish(centred, gram, start, masked):
    local_vars, _, points = masked.shape
    samples, joint = centred.shape
    k = start.shape[1]
    return pl.pallas_call(
        basis_kernel,
        out_shape=(
            jax.ShapeDtypeStruct((local_vars, k, points), BF16),
            jax.ShapeDtypeStruct((samples, k), F32),
            jax.ShapeDtypeStruct((local_vars, samples), F32),
        ),
        in_specs=[pl.BlockSpec(memory_space=pltpu.VMEM)] * 4,
        out_specs=(pl.BlockSpec(memory_space=pltpu.VMEM),) * 3,
        scratch_shapes=[
            pltpu.VMEM((samples, joint), BF16),
            pltpu.VMEM((samples, joint), BF16),
            pltpu.VMEM((joint, joint), BF16),
            pltpu.VMEM((joint, joint), BF16),
            pltpu.VMEM((joint, k), F32),
            pltpu.VMEM((k, k), F32),
        ],
        compiler_params=pltpu.CompilerParams(vmem_limit_bytes=48 * 1024 * 1024),
        name="finish",
    )(centred, gram, start, masked)


def shards(n, nv, fields, eigenfunctions, start, grid_count):
    local_vars, samples, local_points = fields.shape
    first_var = lax.axis_index("var") * local_vars
    counts = lax.dynamic_slice_in_dim(grid_count, first_var, local_vars, 0)
    points = lax.axis_index("space") * local_points + jnp.arange(local_points, dtype=jnp.int32)
    valid = points[None, :] < counts[:, None]
    masked = jnp.where(valid[:, None, :], eigenfunctions, jnp.zeros((), eigenfunctions.dtype))
    centred, gram = gather_scores(n, nv, fields, masked)
    return finish(centred, gram, start, masked)


def solution(mesh):
    return jax.shard_map(
        functools.partial(shards, mesh.shape["space"], mesh.shape["var"]),
        mesh=mesh,
        in_specs=(P("var", None, "space"), P("var", None, "space"), P(), P()),
        out_specs=(P("var", None, "space"), P(), P("var", None)),
        check_vma=False,
    )
```

time: 235 us -> 85.7 us (0.36)
  waiting for transfers between devices: 90.5 us -> 0 us
  Pallas kernels: 0 us -> 82.7 us
  other arithmetic: 59 us -> 1.42 us
  matrix products: 42.6 us -> 0 us
  blocking collectives: 22.2 us -> 0 us
  between operations: 14.4 us -> 0.67 us
  local copies, waits for them, and re-layouts: 5.37 us -> 0.74 us
    pallas_call x0 -> x2, Pallas kernels: none -> 82.7 us  [the longest x1 50.8 us: gather_scores(): pl.pallas_call(functools.partial(gather_kernel, n, nv), out_shape=(jax.Sh...]
    psum x1 -> x0, waiting for transfers between devices: 75.6 us -> none  [shards(): summed = lax.psum(part.reshape(samples, local_vars * M), 'space')]
    another operation x11 -> x0, other arithmetic: 47.4 us -> none  [the longest x6 26.4 us: orthogonalize(): lower = jnp.linalg.cholesky(gram)]
    dot_general x10 -> x0, matrix products: 39.8 us -> none  [the longest x6 15.2 us: product(): jnp.dot(left, right, precision=lax.Precision.HIGHEST, preferred_element_t...]
    psum x1 -> x0, blocking collectives: 22.2 us -> none  [shards(): explained = lax.psum(jnp.stack(partial_gain, axis=0), 'space')]
    all_gather x1 -> x0, waiting for transfers between devices: 14.9 us -> none  [shards(): joint = lax.all_gather(summed, 'var', axis=1, tiled=True)]
    reduce_sum x2 -> x0, other arithmetic: 9.68 us -> none  [the longest x1 7.76 us: shards(): deviation = wide - jnp.mean(wide, axis=0, keepdims=True)]
    unnamed x30 -> x2, local copies, waits for them, and re-layouts: 4.33 us -> 0.01 us
  transfers between devices with their start and end apart: 2 -> 0, of which waited for: 2 -> 0; matrix products, arithmetic and copies ran while one was open for 4% -> 0% of each run, Pallas kernels for 0% -> 0%
where the time goes in v1:
time: 85.7 us; the launch traced here: 85.5 us
  Pallas kernels  82.7 us (96%)
  other arithmetic  1.42 us (2%)
    pallas_call x1, Pallas kernels, gather_scores(): pl.pallas_call(functools.partial(gather_kernel, n, nv), out_shape=(jax.Sh...  50.8 us
    pallas_call x1, Pallas kernels, finish(): pl.pallas_call(basis_kernel, out_shape=(jax.ShapeDtypeStruct((local_vars,...  31.9 us

profile of v1, /device:TPU:0, one launch (start us, length us, event | category | flops | bytes accessed | tf_op | source)
XLA Modules:
  0.0 85.5 jit_solution(16843251813592608550)
XLA Ops:
  0.6 0.7 dynamic_slice.3
  1.4 0.1 broadcast_compare_fusion
  1.5 1.3 %broadcast_select_fusion.masked.masked_ref = bf16[2,64,4096]{2,1,0:T(8,128)(2,1)S(1)} fusion(bf16[2,64,4096]{2,1,0:T(8,128)(2,1)} %param.5, pred[2,4096]{1,0:T(4,128)(4,1)S(1)} %broadcast_compare_fusion), kind=kLoop, calls=%fused_computation | loop fusion | flops 524288 | bytes 2105344 | tf_op jit(solution)/shard_map/jit(_where)/select_n | solution.py:305
  2.8 0.0 copy-start
  2.8 50.8 %gather_scores.1 = (f32[1024,512]{1,0:T(8,128)S(1)}, f32[64,128]{1,0:T(8,128)S(1)}) custom-call(bf16[2,1024,4096]{2,1,0:T(8,128)(2,1)} %fields.1, bf16[2,64,4096]{2,1,0:T(8,128)(2,1)S(1)} %broadcast_select_fusion.masked.masked_ref), custom_call_target="tpu_custom_call" | custom-call | tf_op jit(solution)/shard_map/gather_scores/pallas_call | solution.py:172
  53.6 0.0 copy-done
  53.6 31.9 %finish.1 = (bf16[2,128,4096]{2,1,0:T(8,128)(2,1)}, f32[1024,128]{1,0:T(8,128)}, f32[2,1024]{1,0:T(2,128)}) custom-call(f32[1024,512]{1,0:T(8,128)S(1)} %get-tuple-element.5.centred_ref, f32[64,128]{1,0:T(8,128)S(1)} %get-tuple-element.6.gram_ref, f32[512,128]{1,0:T(8,128)S(1)} %copy-done, bf16[2,64,4096]{2,1,0:T(8,128)(2,1)S(1)} %broadcast_select_fusion.masked.masked_ref), custom_call_target="tpu_custom_call" | custom-call | tf_op jit(solution)/shard_map/finish/pallas_call | solution.py:277
  (1 shorter events, 0.0 us)
Async XLA Ops:
  2.8 50.8 %copy-start = (f32[512,128]{1,0:T(8,128)S(1)}, f32[512,128]{1,0:T(8,128)}, u32[]{:S(2)}) copy-start(f32[512,128]{1,0:T(8,128)} %start_ref.1) | copy-start | bytes 786436

commit v2 on v1

v2 whole, which is shorter than its diff:
```python
import functools

import jax
import jax.numpy as jnp
from jax import lax
from jax.experimental import pallas as pl
from jax.experimental.pallas import tpu as pltpu
from jax.sharding import PartitionSpec as P

M = 64
SWEEPS = 2
MESH = pl.DeviceIdType.MESH
F32 = jnp.float32
BF16 = jnp.bfloat16
HIGHEST = lax.Precision.HIGHEST


def dot(left, right, dims, precision=None):
    return lax.dot_general(left, right, (dims, ((), ())), precision=precision, preferred_element_type=F32)


NN = ((1,), (0,))
NT = ((1,), (1,))
TN = ((0,), (0,))


def split(x):
    high = x.astype(BF16)
    return high, (x - high.astype(F32)).astype(BF16)


def dot3(left, right, dims):
    (lh, ll), (rh, rl) = left, right
    return dot(lh, rh, dims) + (dot(lh, rl, dims) + dot(ll, rh, dims))


def remote(src, dst, send, recv, target):
    return pltpu.make_async_remote_copy(
        src_ref=src, dst_ref=dst, send_sem=send, recv_sem=recv, device_id=target, device_id_type=MESH
    )


def masked_block(count, eigen, first):
    points = first + lax.broadcasted_iota(jnp.int32, (1, eigen.shape[1]), 1)
    return eigen * jnp.where(points < count, 1.0, 0.0).astype(eigen.dtype)


def gather_kernel(
    n, nv, counts, fields, eigen, centred_ref, gram_ref,
    fbuf, weights, part, rbuf, red, gpart, grbuf, gred, gfull, jbuf,
    fsem, asend, arecv, gsend, grecv, hsend, hrecv,
    zsend, zrecv, xsend, xrecv, ysend, yrecv, usend, urecv, wsend, wrecv, psend, precv,
):
    var, me = lax.axis_index("var"), lax.axis_index("space")
    local_vars, samples, local_points = fields.shape
    rows = samples // n
    width = local_vars * M
    half = rows // 2
    na, nz = nv // 2, n // 2
    side, core = var // 2, lax.rem(var, 2)
    depth, lane_y = me // 2, lax.rem(me, 2)
    partner = 2 * side + 1 - core

    def at(i):
        return 2 * lax.rem(depth + 1 + i // 2, nz) + lax.rem(lane_y + 1 + lax.rem(i, 2), 2)

    def fetch(i):
        block = pl.ds(pl.multiple_of(at(i) * rows, rows), rows)
        slot = lax.rem(i, 3)
        return pltpu.make_async_copy(fields.at[:, block, :], fbuf.at[slot], fsem.at[slot])

    fetch(0).start()
    fetch(1).start()

    barrier = pltpu.get_barrier_semaphore()
    for d in range(1, n):
        pl.semaphore_signal(barrier, inc=1, device_id=(var, lax.rem(me + d, n)), device_id_type=MESH)
    for d in range(1, nv):
        pl.semaphore_signal(barrier, inc=1, device_id=(lax.rem(var + d, nv), me), device_id_type=MESH)

    grams = []
    for v in range(local_vars):
        masked = masked_block(counts[var * local_vars + v], eigen[v], me * local_points)
        grams.append(dot(masked, masked, NT))
        weights[:, v * M:(v + 1) * M] = masked.T
    gram = jnp.concatenate(grams, axis=1)
    grows = M // n
    gpart[...] = jnp.zeros_like(gpart)
    for s in range(n):
        gpart[s, 0:grows, :] = gram[s * grows:(s + 1) * grows, :]

    pl.semaphore_wait(barrier, n - 1 + nv - 1)

    def send_part(i):
        return remote(part.at[i], rbuf.at[i], asend.at[i], arecv.at[i], (var, at(i)))

    def send_gram(i):
        return remote(gpart.at[at(i)], grbuf.at[i], gsend.at[i], grecv.at[i], (var, at(i)))

    owner = lax.broadcasted_iota(jnp.int32, (rows, width), 1) // M

    def step(i, carry):
        slot = lax.rem(i, 3)

        @pl.when(i + 2 < n)
        def _():
            fetch(i + 2).start()

        @pl.when(i > 0)
        def _():
            send_part(i - 1).start()
            send_gram(i - 1).start()

        fetch(i).wait()
        scores = dot(fbuf[slot, 0], weights[...], NN)
        for v in range(1, local_vars):
            scores = jnp.where(owner == v, dot(fbuf[slot, v], weights[...], NN), scores)
        part[i] = scores
        return carry

    lax.fori_loop(0, n, step, 0)

    def wait_part(i, carry):
        send_part(i).wait()
        send_gram(i).wait()
        return carry

    lax.fori_loop(0, n - 1, wait_part, 0)

    def block(a, z, y, low=0, size=rows):
        return jbuf.at[
            pl.ds(pl.multiple_of((2 * z + y) * rows + low, size), size),
            pl.ds(pl.multiple_of((2 * a + core) * width, width), width),
        ]

    total = part[n - 1]
    gtotal = gpart[me]
    for i in range(n - 1):
        total = total + rbuf[i]
        gtotal = gtotal + grbuf[i]
    red[...] = total
    gred[...] = gtotal
    block(side, depth, lane_y)[...] = total
    gfull[me] = gtotal

    def from_depth(t):
        return lax.rem(depth - t + nz, nz)

    def send_gfull(d):
        return remote(gred, gfull.at[me], hsend.at[d - 1], hrecv.at[d - 1], (var, lax.rem(me + d, n)))

    def send_z(t):
        target = (var, 2 * lax.rem(depth + t, nz) + lane_y)
        return remote(red, block(side, depth, lane_y), zsend.at[t - 1], zrecv.at[t - 1], target)

    def other(e):
        return lax.rem(side + e, na)

    def back(e):
        return lax.rem(side - e + na, na)

    beside = 1 - lane_y

    def send_x(t, e):
        mine = block(side, from_depth(t), lane_y)
        j = t * (na - 1) + e - 1
        return remote(red if t == 0 else mine, mine, xsend.at[j], xrecv.at[j], (2 * other(e) + core, me))

    def send_y(t):
        mine = block(side, from_depth(t), lane_y)
        return remote(red if t == 0 else mine, mine, ysend.at[t], yrecv.at[t], (var, 2 * depth + beside))

    def relay_y(t, e):
        piece = block(back(e), from_depth(t), lane_y, 0, half)
        j = t * (na - 1) + e - 1
        return remote(piece, piece, usend.at[j], urecv.at[j], (var, 2 * depth + beside))

    def relay_x(t, e):
        piece = block(side, from_depth(t), beside, half, half)
        j = t * (na - 1) + e - 1
        return remote(piece, piece, wsend.at[j], wrecv.at[j], (2 * other(e) + core, me))

    def to_partner(t, e, y):
        piece = block(back(e), from_depth(t), lane_y if y == 0 else beside)
        j = (t * na + e) * 2 + y
        return remote(piece, piece, psend.at[j], precv.at[j], (partner, me))

    for t in range(1, nz):
        send_z(t).start()
    for s in range(nz + 2):
        if s < nz:
            if s > 0:
                send_z(s).wait_recv()
            for e in range(1, na):
                send_x(s, e).start()
            send_y(s).start()
            to_partner(s, 0, 0).start()
            if s == 0:
                for d in range(1, n):
                    send_gfull(d).start()
        if 0 <= s - 1 < nz:
            for e in range(1, na):
                send_x(s - 1, e).wait_recv()
                relay_y(s - 1, e).start()
                to_partner(s - 1, e, 0).start()
            send_y(s - 1).wait_recv()
            for e in range(1, na):
                relay_x(s - 1, e).start()
            to_partner(s - 1, 0, 1).start()
        if 0 <= s - 2 < nz:
            for e in range(1, na):
                relay_y(s - 2, e).wait_recv()
                relay_x(s - 2, e).wait_recv()
                to_partner(s - 2, e, 1).start()
    for d in range(1, n):
        send_gfull(d).wait()
    for t in range(1, nz):
        send_z(t).wait_send()
    for t in range(nz):
        send_y(t).wait_send()
        for e in range(1, na):
            send_x(t, e).wait_send()
            relay_y(t, e).wait_send()
            relay_x(t, e).wait_send()
        for e in range(na):
            for y in range(2):
                to_partner(t, e, y).wait()

    mean = jnp.sum(jbuf[...], axis=0, keepdims=True) / samples
    centred_ref[...] = jbuf[...] - mean
    for s in range(n):
        gram_ref[s * grows:(s + 1) * grows, :] = gfull[s, 0:grows, :]


def gather_scores(n, nv, counts, fields, eigen):
    local_vars, samples, points = fields.shape
    rows = samples // n
    width = local_vars * M
    na, nz = nv // 2, n // 2
    dma = pltpu.SemaphoreType.DMA
    pairs = [n - 1, n - 1, n - 1, nz - 1, nz * (na - 1), nz, nz * (na - 1), nz * (na - 1), 2 * nz * na]
    return pl.pallas_call(
        functools.partial(gather_kernel, n, nv),
        out_shape=(
            jax.ShapeDtypeStruct((samples, nv * width), F32),
            jax.ShapeDtypeStruct((M, width), F32),
        ),
        in_specs=[
            pl.BlockSpec(memory_space=pltpu.SMEM),
            pl.BlockSpec(memory_space=pl.ANY),
            pl.BlockSpec(memory_space=pltpu.VMEM),
        ],
        out_specs=(pl.BlockSpec(memory_space=pltpu.VMEM), pl.BlockSpec(memory_space=pltpu.VMEM)),
        scratch_shapes=[
            pltpu.VMEM((3, local_vars, rows, points), BF16),
            pltpu.VMEM((points, width), BF16),
            pltpu.VMEM((n, rows, width), F32),
            pltpu.VMEM((n - 1, rows, width), F32),
            pltpu.VMEM((rows, width), F32),
            pltpu.VMEM((n, 8, width), F32),
            pltpu.VMEM((n - 1, 8, width), F32),
            pltpu.VMEM((8, width), F32),
            pltpu.VMEM((n, 8, width), F32),
            pltpu.VMEM((samples, nv * width), F32),
            dma((3,)),
            *[dma((count,)) for count in pairs for _ in range(2)],
        ],
        compiler_params=pltpu.CompilerParams(
            collective_id=0, has_side_effects=True, vmem_limit_bytes=48 * 1024 * 1024
        ),
        name="gather_scores",
    )(counts, fields, eigen)


def inverse_factor(gram):
    size = gram.shape[0]
    tiles = size // 8
    rows = [gram[8 * i:8 * i + 8, :] for i in range(tiles)]
    lane = lax.broadcasted_iota(jnp.int32, (8, size), 1)
    sublane = lax.broadcasted_iota(jnp.int32, (8, size), 0)

    def column(tile, k):
        return jnp.broadcast_to(tile[:, k:k + 1], (8, size))

    def spread(tile, j):
        return jnp.broadcast_to(tile[j:j + 1, :], (8, size))

    done = []
    for b in range(tiles):
        base = 8 * b
        inside = (lane >= base) & (lane < base + 8)
        tops = [column(rows[b], base + j) for j in range(8)]
        entry = {(i, j): spread(tops[j], i) for j in range(8) for i in range(j, 8)}
        unit = jnp.where(inside, jnp.where(lane - base == sublane, 1.0, 0.0), rows[b])
        line = [spread(unit, j) for j in range(8)]
        inverse = []
        for j in range(8):
            inverse.append(1.0 / entry[j, j])
            for i in range(j + 1, 8):
                factor = entry[i, j] * inverse[j]
                for q in range(j + 1, i + 1):
                    entry[i, q] = entry[i, q] - factor * entry[q, j]
                line[i] = line[i] - factor * line[j]
        rest = line[0]
        pivot = entry[0, 0]
        for j in range(1, 8):
            rest = jnp.where(sublane == j, line[j], rest)
            pivot = jnp.where(sublane == j, entry[j, j], pivot)
        done.append(jnp.where(lane < base + 8, rest, 0.0) * lax.rsqrt(pivot))
        for i in range(b + 1, tiles):
            new = jnp.where(inside, 0.0, rows[i])
            factors = []
            for j in range(8):
                value = column(rows[i], base + j)
                for p in range(j):
                    value = value - factors[p] * entry[j, p]
                factors.append(value * inverse[j])
            for j in range(8):
                new = new - factors[j] * line[j]
            rows[i] = new
    return done


def basis_kernel(
    counts, centred_ref, gram_ref, start_ref, eigen_ref, loadings_ref, scores_ref, explained_ref,
    high_ref, low_ref, cov_high, cov_low, basis_ref, inverse_ref,
):
    var = lax.axis_index("var")
    samples = centred_ref.shape[0]
    local_vars = eigen_ref.shape[0]
    first_point = lax.axis_index("space") * eigen_ref.shape[2]
    width = local_vars * M
    high, low = split(centred_ref[...])
    high_ref[...] = high
    low_ref[...] = low
    cov = dot3((high, low), (high, low), TN) / (samples - 1)
    cov_high[...], cov_low[...] = split(cov)
    basis_ref[...] = start_ref[...]

    def sweep(_, carry):
        image = dot3((cov_high[...], cov_low[...]), split(basis_ref[...]), NN)
        gram = dot(image, image, TN, HIGHEST)
        for i, tile in enumerate(inverse_factor(gram)):
            inverse_ref[8 * i:8 * i + 8, :] = tile
        basis_ref[...] = dot(image, inverse_ref[...], NT, HIGHEST)
        return carry

    lax.fori_loop(0, SWEEPS, sweep, 0)

    scores = dot3((high_ref[...], low_ref[...]), split(basis_ref[...]), NN)
    scores_ref[...] = scores
    scores_low = scores.astype(BF16)
    own = pl.ds(pl.multiple_of(var * width, width), width)
    basis_low = basis_ref[own, :].astype(BF16)
    own_high, own_low = high_ref[:, own], low_ref[:, own]
    ones = jnp.ones((8, basis_low.shape[1]), F32)
    scores_wide = scores_low.astype(F32)
    for v in range(local_vars):
        mine = basis_low[v * M:(v + 1) * M, :]
        masked = masked_block(counts[var * local_vars + v], eigen_ref[v], first_point)
        loadings_ref[v] = dot(mine, masked, TN).astype(BF16)
        left, right = own_high[:, v * M:(v + 1) * M], own_low[:, v * M:(v + 1) * M]
        cross = dot(left, mine, NN) + dot(right, mine, NN)
        wide = mine.astype(F32)
        inner = dot(gram_ref[:, v * M:(v + 1) * M], wide, NN, HIGHEST)
        square = split(dot(wide, inner, TN, HIGHEST))
        quad = dot(scores_low, square[0], NN) + dot(scores_low, square[1], NN)
        gain = scores_wide * (2.0 * cross - quad)
        summed = dot(ones, gain, NT, HIGHEST) / M
        explained_ref[v:v + 1, :] = summed[0:1, :]


def finish(counts, centred, gram, start, eigen):
    local_vars, _, points = eigen.shape
    samples, joint = centred.shape
    k = start.shape[1]
    return pl.pallas_call(
        basis_kernel,
        out_shape=(
            jax.ShapeDtypeStruct((local_vars, k, points), BF16),
            jax.ShapeDtypeStruct((samples, k), F32),
            jax.ShapeDtypeStruct((local_vars, samples), F32),
        ),
        in_specs=[pl.BlockSpec(memory_space=pltpu.SMEM)] + [pl.BlockSpec(memory_space=pltpu.VMEM)] * 4,
        out_specs=(pl.BlockSpec(memory_space=pltpu.VMEM),) * 3,
        scratch_shapes=[
            pltpu.VMEM((samples, joint), BF16),
            pltpu.VMEM((samples, joint), BF16),
            pltpu.VMEM((joint, joint), BF16),
            pltpu.VMEM((joint, joint), BF16),
            pltpu.VMEM((joint, k), F32),
            pltpu.VMEM((k, k), F32),
        ],
        compiler_params=pltpu.CompilerParams(vmem_limit_bytes=48 * 1024 * 1024),
        name="finish",
    )(counts, centred, gram, start, eigen)


def shards(n, nv, fields, eigenfunctions, start, grid_count):
    centred, gram = gather_scores(n, nv, grid_count, fields, eigenfunctions)
    return finish(grid_count, centred, gram, start, eigenfunctions)


def solution(mesh):
    return jax.shard_map(
        functools.partial(shards, mesh.shape["space"], mesh.shape["var"]),
        mesh=mesh,
        in_specs=(P("var", None, "space"), P("var", None, "space"), P(), P()),
        out_specs=(P("var", None, "space"), P(), P("var", None)),
        check_vma=False,
    )
```

time: 85.7 us -> 61.9 us (0.72)
  Pallas kernels: 82.7 us -> 59.1 us
  other arithmetic: 1.42 us -> 0 us
  local copies, waits for them, and re-layouts: 0.74 us -> 1.88 us
    pallas_call x1, Pallas kernels: 31.9 us -> 20.1 us  [finish(): pl.pallas_call(basis_kernel, out_shape=(jax.ShapeDtypeStruct((local_vars,...]
    pallas_call x1, Pallas kernels: 50.8 us -> 39 us  [gather_scores(): pl.pallas_call(functools.partial(gather_kernel, n, nv), out_shape=(jax.Sh...]
    unnamed x2 -> x6, local copies, waits for them, and re-layouts: 0.01 us -> 1.88 us
    select_n x1 -> x0, other arithmetic: 1.33 us -> none  [shards(): jnp.where(valid[:, None, :], eigenfunctions, jnp.zeros((), eigenfunctions...]
where the time goes in v2:
time: 61.9 us; the launch traced here: 61.7 us
  Pallas kernels  59.1 us (95%)
  local copies, waits for them, and re-layouts  1.88 us (3%)
  between operations  0.66 us (1%)
    pallas_call x1, Pallas kernels, gather_scores(): pl.pallas_call(functools.partial(gather_kernel, n, nv), out_shape=(jax.Sh...  39 us
    pallas_call x1, Pallas kernels, finish(): pl.pallas_call(basis_kernel, out_shape=(jax.ShapeDtypeStruct((local_vars,...  20.1 us
    unnamed x6, local copies, waits for them, and re-layouts  1.88 us

profile of v2, /device:TPU:0, one launch (start us, length us, event | category | flops | bytes accessed | tf_op | source)
XLA Modules:
  0.0 61.7 jit_solution(6792998921546239655)
XLA Ops:
  0.6 0.0 copy-start
  0.6 1.2 %copy-done = bf16[2,64,4096]{2,1,0:T(8,128)(2,1)S(1)} copy-done((bf16[2,64,4096]{2,1,0:T(8,128)(2,1)S(1)}, bf16[2,64,4096]{2,1,0:T(8,128)(2,1)}, u32[]{:S(2)}) %copy-start) | copy-done | bytes 1048600
  1.9 0.0 copy-start.2
  1.9 0.7 %copy-done.2 = s32[8]{0:T(128)S(1)} copy-done((s32[8]{0:T(128)S(1)}, s32[8]{0:T(128)}, u32[]{:S(2)}) %copy-start.2) | copy-done | bytes 56
  2.5 0.0 copy-start.1
  2.5 39.0 %gather_scores.1 = (f32[1024,512]{1,0:T(8,128)S(1)}, f32[64,128]{1,0:T(8,128)S(1)}) custom-call(s32[8]{0:T(128)S(1)} %copy-done.2, bf16[2,1024,4096]{2,1,0:T(8,128)(2,1)} %fields.1, bf16[2,64,4096]{2,1,0:T(8,128)(2,1)S(1)} %copy-done), custom_call_target="tpu_custom_call" | custom-call | tf_op jit(solution)/shard_map/gather_scores/pallas_call | solution.py:242
  41.6 0.0 copy-done.1
  41.6 20.1 %finish.1 = (bf16[2,128,4096]{2,1,0:T(8,128)(2,1)}, f32[1024,128]{1,0:T(8,128)}, f32[2,1024]{1,0:T(2,128)}) custom-call(s32[8]{0:T(128)S(1)} %copy-done.2, f32[1024,512]{1,0:T(8,128)S(1)} %get-tuple-element.5.centred_ref, f32[64,128]{1,0:T(8,128)S(1)} %get-tuple-element.6.gram_ref, f32[512,128]{1,0:T(8,128)S(1)} %copy-done.1, bf16[2,64,4096]{2,1,0:T(8,128)(2,1)S(1)} %copy-done), custom_call_target="tpu_custom_call" | custom-call | tf_op jit(solution)/shard_map/finish/pallas_call | solution.py:377
Async XLA Ops:
  0.6 1.2 %copy-start = (bf16[2,64,4096]{2,1,0:T(8,128)(2,1)S(1)}, bf16[2,64,4096]{2,1,0:T(8,128)(2,1)}, u32[]{:S(2)}) copy-start(bf16[2,64,4096]{2,1,0:T(8,128)(2,1)} %eigen_ref.1) | copy-start | bytes 3145732
  1.9 0.7 %copy-start.2 = (s32[8]{0:T(128)S(1)}, s32[8]{0:T(128)}, u32[]{:S(2)}) copy-start(s32[8]{0:T(128)} %counts.3) | copy-start | bytes 100
  2.5 39.1 %copy-start.1 = (f32[512,128]{1,0:T(8,128)S(1)}, f32[512,128]{1,0:T(8,128)}, u32[]{:S(2)}) copy-start(f32[512,128]{1,0:T(8,128)} %start_ref.1) | copy-start | bytes 786436

commit v3 on v2

--- a/solution.py
+++ b/solution.py
@@ -46,8 +46,8 @@
 
 
 def gather_kernel(
-    n, nv, counts, fields, eigen, centred_ref, gram_ref,
-    fbuf, weights, part, rbuf, red, gpart, grbuf, gred, gfull, jbuf,
+    n, nv, counts, fields, eigen_far, centred_ref, gram_ref,
+    eigen, esem, fbuf, weights, part, rbuf, red, gpart, grbuf, gred, gfull, jbuf,
     fsem, asend, arecv, gsend, grecv, hsend, hrecv,
     zsend, zrecv, xsend, xrecv, ysend, yrecv, usend, urecv, wsend, wrecv, psend, precv,
 ):
@@ -66,11 +66,12 @@
 
     def fetch(i):
         block = pl.ds(pl.multiple_of(at(i) * rows, rows), rows)
-        slot = lax.rem(i, 3)
-        return pltpu.make_async_copy(fields.at[:, block, :], fbuf.at[slot], fsem.at[slot])
-
-    fetch(0).start()
-    fetch(1).start()
+        return pltpu.make_async_copy(fields.at[:, block, :], fbuf.at[i], fsem.at[i])
+
+    eigen_copy = pltpu.make_async_copy(eigen_far, eigen, esem)
+    eigen_copy.start()
+    for i in range(n):
+        fetch(i).start()
 
     barrier = pltpu.get_barrier_semaphore()
     for d in range(1, n):
@@ -78,6 +79,7 @@
     for d in range(1, nv):
         pl.semaphore_signal(barrier, inc=1, device_id=(lax.rem(var + d, nv), me), device_id_type=MESH)
 
+    eigen_copy.wait()
     grams = []
     for v in range(local_vars):
         masked = masked_block(counts[var * local_vars + v], eigen[v], me * local_points)
@@ -100,21 +102,15 @@
     owner = lax.broadcasted_iota(jnp.int32, (rows, width), 1) // M
 
     def step(i, carry):
-        slot = lax.rem(i, 3)
-
-        @pl.when(i + 2 < n)
-        def _():
-            fetch(i + 2).start()
-
         @pl.when(i > 0)
         def _():
             send_part(i - 1).start()
             send_gram(i - 1).start()
 
         fetch(i).wait()
-        scores = dot(fbuf[slot, 0], weights[...], NN)
+        scores = dot(fbuf[i, 0], weights[...], NN)
         for v in range(1, local_vars):
-            scores = jnp.where(owner == v, dot(fbuf[slot, v], weights[...], NN), scores)
+            scores = jnp.where(owner == v, dot(fbuf[i, v], weights[...], NN), scores)
         part[i] = scores
         return carry
 
@@ -247,12 +243,14 @@
         ),
         in_specs=[
             pl.BlockSpec(memory_space=pltpu.SMEM),
-            pl.BlockSpec(memory_space=pl.ANY),
-            pl.BlockSpec(memory_space=pltpu.VMEM),
+            pl.BlockSpec(memory_space=pltpu.HBM),
+            pl.BlockSpec(memory_space=pltpu.HBM),
         ],
         out_specs=(pl.BlockSpec(memory_space=pltpu.VMEM), pl.BlockSpec(memory_space=pltpu.VMEM)),
         scratch_shapes=[
-            pltpu.VMEM((3, local_vars, rows, points), BF16),
+            pltpu.VMEM((local_vars, M, points), BF16),
+            dma,
+            pltpu.VMEM((n, local_vars, rows, points), BF16),
             pltpu.VMEM((points, width), BF16),
             pltpu.VMEM((n, rows, width), F32),
             pltpu.VMEM((n - 1, rows, width), F32),
@@ -262,11 +260,11 @@
             pltpu.VMEM((8, width), F32),
             pltpu.VMEM((n, 8, width), F32),
             pltpu.VMEM((samples, nv * width), F32),
-            dma((3,)),
+            dma((n,)),
             *[dma((count,)) for count in pairs for _ in range(2)],
         ],
         compiler_params=pltpu.CompilerParams(
-            collective_id=0, has_side_effects=True, vmem_limit_bytes=48 * 1024 * 1024
+            collective_id=0, has_side_effects=True, vmem_limit_bytes=61 * 1024 * 1024
         ),
         name="gather_scores",
     )(counts, fields, eigen)
@@ -322,9 +320,13 @@
 
 
 def basis_kernel(
-    counts, centred_ref, gram_ref, start_ref, eigen_ref, loadings_ref, scores_ref, explained_ref,
-    high_ref, low_ref, cov_high, cov_low, basis_ref, inverse_ref,
+    counts, centred_ref, gram_ref, start_far, eigen_far, loadings_ref, scores_ref, explained_ref,
+    high_ref, low_ref, cov_high, cov_low, basis_ref, inverse_ref, eigen_ref, start_sem, eigen_sem,
 ):
+    start_copy = pltpu.make_async_copy(start_far, basis_ref, start_sem)
+    eigen_copy = pltpu.make_async_copy(eigen_far, eigen_ref, eigen_sem)
+    start_copy.start()
+    eigen_copy.start()
     var = lax.axis_index("var")
     samples = centred_ref.shape[0]
     local_vars = eigen_ref.shape[0]
@@ -335,7 +337,7 @@
     low_ref[...] = low
     cov = dot3((high, low), (high, low), TN) / (samples - 1)
     cov_high[...], cov_low[...] = split(cov)
-    basis_ref[...] = start_ref[...]
+    start_copy.wait()
 
     def sweep(_, carry):
         image = dot3((cov_high[...], cov_low[...]), split(basis_ref[...]), NN)
@@ -353,6 +355,7 @@
     own = pl.ds(pl.multiple_of(var * width, width), width)
     basis_low = basis_ref[own, :].astype(BF16)
     own_high, own_low = high_ref[:, own], low_ref[:, own]
+    eigen_copy.wait()
     ones = jnp.ones((8, basis_low.shape[1]), F32)
     scores_wide = scores_low.astype(F32)
     for v in range(local_vars):
@@ -381,7 +384,9 @@
             jax.ShapeDtypeStruct((samples, k), F32),
             jax.ShapeDtypeStruct((local_vars, samples), F32),
         ),
-        in_specs=[pl.BlockSpec(memory_space=pltpu.SMEM)] + [pl.BlockSpec(memory_space=pltpu.VMEM)] * 4,
+        in_specs=[pl.BlockSpec(memory_space=pltpu.SMEM)]
+        + [pl.BlockSpec(memory_space=pltpu.VMEM)] * 2
+        + [pl.BlockSpec(memory_space=pltpu.HBM)] * 2,
         out_specs=(pl.BlockSpec(memory_space=pltpu.VMEM),) * 3,
         scratch_shapes=[
             pltpu.VMEM((samples, joint), BF16),
@@ -390,8 +395,11 @@
             pltpu.VMEM((joint, joint), BF16),
             pltpu.VMEM((joint, k), F32),
             pltpu.VMEM((k, k), F32),
+            pltpu.VMEM((local_vars, M, points), BF16),
+            pltpu.SemaphoreType.DMA,
+            pltpu.SemaphoreType.DMA,
         ],
-        compiler_params=pltpu.CompilerParams(vmem_limit_bytes=48 * 1024 * 1024),
+        compiler_params=pltpu.CompilerParams(vmem_limit_bytes=61 * 1024 * 1024),
         name="finish",
     )(counts, centred, gram, start, eigen)
 

time: 61.9 us -> 67.8 us (1.095)
  Pallas kernels: 59.1 us -> 66.8 us
  local copies, waits for them, and re-layouts: 1.88 us -> 0 us
    pallas_call x1, Pallas kernels: 39 us -> 44.3 us  [gather_scores(): pl.pallas_call(functools.partial(gather_kernel, n, nv), out_shape=(jax.Sh...]
    pallas_call x1, Pallas kernels: 20.1 us -> 22.5 us  [finish(): pl.pallas_call(basis_kernel, out_shape=(jax.ShapeDtypeStruct((local_vars,...]
    unnamed x6 -> x0, local copies, waits for them, and re-layouts: 1.88 us -> none
where the time goes in v3:
time: 67.8 us; the launch traced here: 67.4 us
  Pallas kernels  66.8 us (99%)
    pallas_call x1, Pallas kernels, gather_scores(): pl.pallas_call(functools.partial(gather_kernel, n, nv), out_shape=(jax.Sh...  44.3 us
    pallas_call x1, Pallas kernels, finish(): pl.pallas_call(basis_kernel, out_shape=(jax.ShapeDtypeStruct((local_vars,...  22.5 us

profile of v3, /device:TPU:0, one launch (start us, length us, event | category | flops | bytes accessed | tf_op | source)
XLA Modules:
  0.0 67.4 jit_solution(16234665177909842766)
XLA Ops:
  0.6 44.3 %gather_scores.1 = (f32[1024,512]{1,0:T(8,128)}, f32[64,128]{1,0:T(8,128)}) custom-call(s32[8]{0:T(128)} %counts.3, bf16[2,1024,4096]{2,1,0:T(8,128)(2,1)} %fields.1, bf16[2,64,4096]{2,1,0:T(8,128)(2,1)} %eigen_far.3), custom_call_target="tpu_custom_call" | custom-call | tf_op jit(solution)/shard_map/gather_scores/pallas_call | solution.py:238
  45.0 22.5 %finish.1 = (bf16[2,128,4096]{2,1,0:T(8,128)(2,1)}, f32[1024,128]{1,0:T(8,128)}, f32[2,1024]{1,0:T(2,128)}) custom-call(s32[8]{0:T(128)} %counts.3, f32[1024,512]{1,0:T(8,128)} %get-tuple-element.5.centred_ref, f32[64,128]{1,0:T(8,128)} %get-tuple-element.6.gram_ref, f32[512,128]{1,0:T(8,128)} %start_far.1, bf16[2,64,4096]{2,1,0:T(8,128)(2,1)} %eigen_far.3), custom_call_target="tpu_custom_call" | custom-call | tf_op jit(solution)/shard_map/finish/pallas_call | solution.py:380
